TPU v7x, 32 devices: a whole 2x2x4 slice. The times are simulated.
32 devices in a mesh: section: 4 (over x, core), seq: 8 (over z, y).
Axes of the slice: x: 2, y: 2, z: 4, core: 2. Of those that a mesh axis runs over, the one named last changes fastest.
Arguments:
- layer_input: bfloat16 [4, 512, 4, 1536], P('section', 'seq'), may hold values from -300 to 300
- norm_gain: float32 [4, 1536], P('section'), may hold values from 0.1 to 1.9
- queries: bfloat16 [4, 512, 4, 1024], P('section', 'seq'), may hold values from -6 to 6
- key_states: bfloat16 [4, 512, 4, 1024], P('section', 'seq'), may hold values from -6 to 6
- value_states: bfloat16 [4, 512, 4, 1024], P('section', 'seq'), may hold values from -6 to 6
- out_grad: bfloat16 [4, 512, 4, 1536], P('section', 'seq'), may hold values from -6 to 6
- out_weight: bfloat16 [4, 1024, 1536], P('section', 'seq'), may hold values from -0.1875 to 0.1875
- qkv_weight: bfloat16 [4, 1536, 3072], P('section', 'seq'), may hold values from -0.15625 to 0.15625
- lengths: int32 [4, 4], P('section'), may hold values from 256 to 512
Outputs:
- passed_grad: bfloat16 [4, 512, 4, 1536], P('section', 'seq')
All inputs are finite; a program needn't handle non-finite values.
Results may differ from a plain program's by a relative error of at most 0.0034.
Values may be sent and summed in bfloat16 or wider, within the bound.
A program may use at most 128 MiB of HBM per device.

v0:
```python
import jax
import jax.numpy as jnp
from jax import lax
from jax.sharding import PartitionSpec as P

HEADS = 16
HS = 64


EPSILON = 1e-05
MASKED = -1e30
ROW_DOT = (((1,), (1,)), ((), ()))
COL_DOT = (((0,), (0,)), ((), ()))


def shifted(shard, axis, by):
    count = lax.axis_size(axis)
    return lax.ppermute(shard, axis, [(i, (i + by) % count) for i in range(count)])


def item_backward(query_rows, key_rows, value_rows, grad_rows, key_valid):
    length = query_rows.shape[0]
    block = min(512, length)
    scale = HS ** (-0.5)
    offsets = jnp.arange(0, length, block)
    zeros = jnp.zeros((length, query_rows.shape[1]), jnp.float32)

    def step(carry, offset):
        key_total, value_total = carry
        query_block = lax.dynamic_slice_in_dim(query_rows, offset, block, 0)
        grad_block = lax.dynamic_slice_in_dim(grad_rows, offset, block, 0)
        scores = (
            lax.dot_general(query_block, key_rows, ROW_DOT, preferred_element_type=jnp.float32)
            * scale
        )
        scores = jnp.where(key_valid[None, :], scores, MASKED)
        largest = jnp.max(scores, axis=1, keepdims=True)
        weights = jnp.exp(scores - largest)
        probs = weights / jnp.sum(weights, axis=1, keepdims=True)
        probs_low = probs.astype(jnp.bfloat16)
        grad_probs = lax.dot_general(
            grad_block, value_rows, ROW_DOT, preferred_element_type=jnp.float32
        )
        centre = jnp.sum(probs * grad_probs, axis=1, keepdims=True)
        grad_scores = (probs * (grad_probs - centre) * scale).astype(jnp.bfloat16)
        query_grad = jnp.dot(grad_scores, key_rows, preferred_element_type=jnp.float32)
        key_total = key_total + lax.dot_general(
            grad_scores, query_block, COL_DOT, preferred_element_type=jnp.float32
        )
        value_total = value_total + lax.dot_general(
            probs_low, grad_block, COL_DOT, preferred_element_type=jnp.float32
        )
        return ((key_total, value_total), query_grad.astype(jnp.bfloat16))

    (key_total, value_total), query_parts = lax.scan(step, (zeros, zeros), offsets)
    query_grad = query_parts.reshape(length, query_rows.shape[1])
    return (query_grad, key_total.astype(jnp.bfloat16), value_total.astype(jnp.bfloat16))


def split_items(columns):
    length = columns.shape[0]
    count = columns.shape[1] // HS
    return columns.reshape(length, count, HS).transpose(1, 0, 2)


def join_items(items):
    count = items.shape[0]
    length = items.shape[1]
    return items.transpose(1, 0, 2).reshape(length, count * HS)


def project_grad(flat_grad, out_rows):
    return lax.dot_general(
        flat_grad,
        lax.all_gather(out_rows, "seq", axis=0, tiled=True),
        ROW_DOT,
        preferred_element_type=jnp.float32,
    ).astype(jnp.bfloat16)


def on_device(
    layer_input,
    norm_gain,
    queries,
    key_states,
    value_states,
    out_grad,
    out_weight,
    qkv_weight,
    lengths,
):
    frames = queries.shape[1]
    records = queries.shape[2]
    features = queries.shape[3]
    model_width = out_grad.shape[3]
    flat_grad = out_grad[0].reshape(frames * records, model_width)
    frame_queries = queries[0].reshape(frames, records * features)
    frame_keys = key_states[0].reshape(frames, records * features)
    frame_values = value_states[0].reshape(frames, records * features)
    attn_grad = project_grad(flat_grad, out_weight[0])
    head_queries, head_keys, head_values, head_grads = (
        lax.all_to_all(frame_queries, "seq", split_axis=1, concat_axis=0, tiled=True),
        lax.all_to_all(frame_keys, "seq", split_axis=1, concat_axis=0, tiled=True),
        lax.all_to_all(frame_values, "seq", split_axis=1, concat_axis=0, tiled=True),
        lax.all_to_all(
            attn_grad.reshape(frames, records * features),
            "seq",
            split_axis=1,
            concat_axis=0,
            tiled=True,
        ),
    )
    items_here = head_queries.shape[1] // HS
    length = head_queries.shape[0]
    item_ids = lax.axis_index("seq") * items_here + jnp.arange(items_here, dtype=jnp.int32)
    record_ids = item_ids // HEADS
    record_pick = jnp.arange(records, dtype=jnp.int32)[None, :] == record_ids[:, None]
    item_lengths = jnp.sum(jnp.where(record_pick, lengths[0][None, :], 0), axis=1)
    key_valid = jnp.arange(length, dtype=jnp.int32)[None, :] < item_lengths[:, None]
    query_grad, key_gradient, value_grad = lax.map(
        lambda group: item_backward(*group),
        (
            split_items(head_queries),
            split_items(head_keys),
            split_items(head_values),
            split_items(head_grads),
            key_valid,
        ),
    )
    query_back, key_backward, value_back = (
        lax.all_to_all(join_items(query_grad), "seq", split_axis=0, concat_axis=1, tiled=True),
        lax.all_to_all(join_items(key_gradient), "seq", split_axis=0, concat_axis=1, tiled=True),
        lax.all_to_all(join_items(value_grad), "seq", split_axis=0, concat_axis=1, tiled=True),
    )
    joined = jnp.concatenate(
        [
            query_back.reshape(frames * records, features),
            key_backward.reshape(frames * records, features),
            value_back.reshape(frames * records, features),
        ],
        axis=1,
    )
    norm_grad = lax.dot_general(
        joined,
        lax.all_gather(qkv_weight[0], "seq", axis=0, tiled=True),
        ROW_DOT,
        preferred_element_type=jnp.float32,
    )
    inputs = layer_input[0].reshape(frames * records, model_width).astype(jnp.float32)
    row_average = jnp.mean(inputs, axis=1, keepdims=True)
    centered_input = inputs - row_average
    var = jnp.mean(centered_input * centered_input, axis=1, keepdims=True)
    inverse_deviation = 1.0 / jnp.sqrt(var + EPSILON)
    normalized_input = centered_input * inverse_deviation
    scaled_rows = norm_grad * norm_gain[0][None, :]
    residual_branch = inverse_deviation * (
        scaled_rows
        - jnp.mean(scaled_rows, axis=1, keepdims=True)
        - normalized_input * jnp.mean(scaled_rows * normalized_input, axis=1, keepdims=True)
    )
    input_grad = (flat_grad.astype(jnp.float32) + residual_branch).astype(jnp.bfloat16)
    input_grad = input_grad.reshape(1, frames, records, model_width)
    return shifted(input_grad, "section", -1)


def solution(mesh):
    in_specs = (
        P("section", "seq", None, None),
        P("section", None),
        P("section", "seq", None, None),
        P("section", "seq", None, None),
        P("section", "seq", None, None),
        P("section", "seq", None, None),
        P("section", "seq", None),
        P("section", "seq", None),
        P("section", None),
    )
    out_specs = P("section", "seq", None, None)
    return jax.shard_map(
        on_device, mesh=mesh, in_specs=in_specs, out_specs=out_specs, check_vma=False
    )
```

profile of v0, /device:TPU:27, one launch (start us, length us, event | category | flops | bytes accessed | tf_op | source)
XLA Modules:
  0.0 298.9 jit_solution(11840325789857754773)
XLA Ops:
  9.4 5.5 %all-to-all-start = ((bf16[64,8,512]{2,0,1:T(8,128)(2,1)}), bf16[64,8,512]{2,0,1:T(8,128)(2,1)S(1)}, u32[]{:S(2)}, u32[]{:S(2)}) async-start(bf16[64,8,512]{2,0,1:T(8,128)(2,1)} %copy.24), calls=%async_computation | async-start | bytes 1048576 | tf_op jit(solution)/shard_map/all_to_all | solution.py:102
  16.0 17.5 %all-to-all-done = bf16[64,8,512]{2,0,1:T(8,128)(2,1)S(1)} async-done(((bf16[64,8,512]{2,0,1:T(8,128)(2,1)}), bf16[64,8,512]{2,0,1:T(8,128)(2,1)S(1)}, u32[]{:S(2)}, u32[]{:S(2)}) %all-to-all-start) | async-done | bytes 524320 | tf_op jit(solution)/shard_map/all_to_all | solution.py:102
  33.5 9.6 %all-to-all-start.1 = ((bf16[64,8,512]{2,0,1:T(8,128)(2,1)}), bf16[64,8,512]{2,0,1:T(8,128)(2,1)S(1)}, u32[]{:S(2)}, u32[]{:S(2)}) async-start(bf16[64,8,512]{2,0,1:T(8,128)(2,1)} %copy.25), calls=%async_computation.1 | async-start | bytes 1048576 | tf_op jit(solution)/shard_map/all_to_all | solution.py:103
  44.2 19.7 %all-to-all-done.1 = bf16[64,8,512]{2,0,1:T(8,128)(2,1)S(1)} async-done(((bf16[64,8,512]{2,0,1:T(8,128)(2,1)}), bf16[64,8,512]{2,0,1:T(8,128)(2,1)S(1)}, u32[]{:S(2)}, u32[]{:S(2)}) %all-to-all-start.1) | async-done | bytes 524320 | tf_op jit(solution)/shard_map/all_to_all | solution.py:103
  63.9 9.9 %all-to-all-start.3 = ((bf16[64,8,512]{2,0,1:T(8,128)(2,1)}), bf16[64,8,512]{2,0,1:T(8,128)(2,1)S(1)}, u32[]{:S(2)}, u32[]{:S(2)}) async-start(bf16[64,8,512]{2,0,1:T(8,128)(2,1)} %copy.27), calls=%async_computation.3 | async-start | bytes 1048576 | tf_op jit(solution)/shard_map/all_to_all | solution.py:104
  74.0 16.5 %all-gather.5.cloned.1.call-done = bf16[1,1024,1536]{2,1,0:T(8,128)(2,1)} async-done(((bf16[1,128,1536]{2,1,0:T(8,128)(2,1)}), bf16[1,1024,1536]{2,1,0:T(8,128)(2,1)}) %all-gather.5.cloned.1.call-update) | async-done | bytes 3145744 | tf_op jit(solution)/shard_map/all_gather | solution.py:75
  90.5 2.9 fusion.43
  94.6 6.5 %all-to-all-start.2 = ((bf16[64,8,512]{2,0,1:T(8,128)(2,1)}), bf16[64,8,512]{2,0,1:T(8,128)(2,1)}, u32[]{:S(2)}, u32[]{:S(2)}) async-start(bf16[64,8,512]{2,0,1:T(8,128)(2,1)} %copy.26), calls=%async_computation.2 | async-start | bytes 1048576 | tf_op jit(solution)/shard_map/all_to_all | solution.py:105
  102.7 1.6 reshape.134
  104.5 1.6 reshape.136
  107.3 6.4 %all-to-all-done.2 = bf16[64,8,512]{2,0,1:T(8,128)(2,1)} async-done(((bf16[64,8,512]{2,0,1:T(8,128)(2,1)}), bf16[64,8,512]{2,0,1:T(8,128)(2,1)}, u32[]{:S(2)}, u32[]{:S(2)}) %all-to-all-start.2) | async-done | bytes 524320 | tf_op jit(solution)/shard_map/all_to_all | solution.py:105
  113.7 1.7 reshape.135
  116.5 46.3 %while.14 = (s32[]{:T(128)}, bf16[8,512,64]{1,2,0:T(8,128)(2,1)}, bf16[8,512,64]{1,2,0:T(8,128)(2,1)}, bf16[8,512,64]{1,2,0:T(8,128)(2,1)}, pred[8,512]{1,0:T(8,...) while((s32[]{:T(128)}, bf16[8,512,64]{1,2,0:T(8,128)(2,1)}, ...), condition=%wide.region_7.8_spmd, body=%wide.region_3.7_spmd.sunk | while | flops 172587520 | bytes 10056297 | solution.py:120
  117.1 1.8 fusion.73
  122.9 1.8 fusion.73
  128.6 1.9 fusion.73
  134.4 1.9 fusion.73
  140.2 1.9 fusion.73
  146.0 1.8 fusion.73
  151.8 1.8 fusion.73
  157.6 1.8 fusion.73
  162.9 1.7 reshape.144
  164.6 1.5 copy.38
  166.1 5.9 %all-to-all-start.4 = ((bf16[8,64,512]{2,1,0:T(8,128)(2,1)}), bf16[8,64,512]{2,1,0:T(8,128)(2,1)S(1)}, u32[]{:S(2)}, u32[]{:S(2)}) async-start(bf16[8,64,512]{2,1,0:T(8,128)(2,1)} %copy.38), calls=%async_computation.4 | async-start | bytes 1048576 | tf_op jit(solution)/shard_map/all_to_all | solution.py:131
  174.0 26.1 %all-to-all-done.4 = bf16[8,64,512]{2,1,0:T(8,128)(2,1)S(1)} async-done(((bf16[8,64,512]{2,1,0:T(8,128)(2,1)}), bf16[8,64,512]{2,1,0:T(8,128)(2,1)S(1)}, u32[]{:S(2)}, u32[]{:S(2)}) %all-to-all-start.4) | async-done | bytes 524320 | tf_op jit(solution)/shard_map/all_to_all | solution.py:131
  200.1 5.4 %all-to-all-start.5 = ((bf16[8,64,512]{2,1,0:T(8,128)(2,1)}), bf16[8,64,512]{2,1,0:T(8,128)(2,1)S(1)}, u32[]{:S(2)}, u32[]{:S(2)}) async-start(bf16[8,64,512]{2,1,0:T(8,128)(2,1)} %copy.39), calls=%async_computation.5 | async-start | bytes 1048576 | tf_op jit(solution)/shard_map/all_to_all | solution.py:132
  207.5 25.9 %all-to-all-done.5 = bf16[8,64,512]{2,1,0:T(8,128)(2,1)S(1)} async-done(((bf16[8,64,512]{2,1,0:T(8,128)(2,1)}), bf16[8,64,512]{2,1,0:T(8,128)(2,1)S(1)}, u32[]{:S(2)}, u32[]{:S(2)}) %all-to-all-start.5) | async-done | bytes 524320 | tf_op jit(solution)/shard_map/all_to_all | solution.py:132
  233.4 5.4 %all-to-all-start.6 = ((bf16[8,64,512]{2,1,0:T(8,128)(2,1)}), bf16[8,64,512]{2,1,0:T(8,128)(2,1)}, u32[]{:S(2)}, u32[]{:S(2)}) async-start(bf16[8,64,512]{2,1,0:T(8,128)(2,1)} %copy.40), calls=%async_computation.6 | async-start | bytes 1048576 | tf_op jit(solution)/shard_map/all_to_all | solution.py:133
  242.0 21.3 %all-to-all-done.6 = bf16[8,64,512]{2,1,0:T(8,128)(2,1)} async-done(((bf16[8,64,512]{2,1,0:T(8,128)(2,1)}), bf16[8,64,512]{2,1,0:T(8,128)(2,1)}, u32[]{:S(2)}, u32[]{:S(2)}) %all-to-all-start.6) | async-done | bytes 524320 | tf_op jit(solution)/shard_map/all_to_all | solution.py:133
  265.6 6.5 %all-gather.7.cloned.1.call-done = bf16[1,1536,3072]{2,1,0:T(8,128)(2,1)} async-done(((bf16[1,192,3072]{2,1,0:T(8,128)(2,1)}), bf16[1,1536,3072]{2,1,0:T(8,128)(2,1)}) %all-gather.7.cloned.1.call-update) | async-done | bytes 9437200 | tf_op jit(solution)/shard_map/all_gather | solution.py:145
  272.1 6.7 %fusion.47 = (f32[256]{0:T(256)S(1)}, f32[256]{0:T(256)S(1)}, f32[256,1536]{1,0:T(8,128)S(1)}) fusion(f32[256]{0:T(256)S(1)} %sqrt.6, f32[256,1536]{1,0:T(8,128)S(1)} %reshape.141, f32[256]{0:T(256)S(1)} %div.47, f32[1536]{0:T(1024)S(1)} %reduce.3, bf16[1,1536,3072]{2,1,0:T(8,128)(2,1)} %all-gather.7.cloned.1.call-done, bf16[256,1024]{1,0:T(8,128)(2,1)} %reshape.139, ...), kind=kOutput, calls=%fused_computation.66 | convolution fusion | flops 2422996480 | bytes 14166016 | tf_op jit(solution)/shard_map/dot_general | solution.py:143
  280.3 10.9 %collective-permute-done = bf16[1,64,4,1536]{3,2,1,0:T(4,128)(2,1)S(1)} collective-permute-done((bf16[1,64,4,1536]{3,2,1,0:T(4,128)(2,1)S(1)}, bf16[1,64,4,1536]{3,2,1,0:T(4,128)(2,1)S(1)}, u32[]{:S(2)}, u32[]{:S(2)}) %collective-permute-start) | collective-permute-done | bytes 786464 | tf_op jit(solution)/shard_map/ppermute | solution.py:18
  (130 shorter events, 53.6 us)
Async XLA Ops:
  6.5 84.0 %all-gather.5.cloned.1.call-start = ((), (), s32[]{:S(2)}) async-start(), calls=%async_computation.7 | async-start | bytes 3538944 | tf_op jit(solution)/shard_map/all_gather | solution.py:75
  7.3 7.7 %copy-start.8 = (bf16[1,64,4,1024]{3,2,1,0:T(4,128)(2,1)S(1)}, bf16[1,64,4,1024]{3,2,1,0:T(4,128)(2,1)}, u32[]{:S(2)}) copy-start(bf16[1,64,4,1024]{3,2,1,0:T(4,128)(2,1)} %param.14) | copy-start | bytes 1572868
  9.4 24.1 %all-to-all-start = ((bf16[64,8,512]{2,0,1:T(8,128)(2,1)}), bf16[64,8,512]{2,0,1:T(8,128)(2,1)S(1)}, u32[]{:S(2)}, u32[]{:S(2)}) async-start(bf16[64,8,512]{2,0,1:T(8,128)(2,1)} %copy.24), calls=%async_computation | async-start | bytes 1048576 | tf_op jit(solution)/shard_map/all_to_all | solution.py:102
  14.9 28.2 %copy-start.9 = (bf16[1,64,4,1024]{3,2,1,0:T(4,128)(2,1)S(1)}, bf16[1,64,4,1024]{3,2,1,0:T(4,128)(2,1)}, u32[]{:S(2)}) copy-start(bf16[1,64,4,1024]{3,2,1,0:T(4,128)(2,1)} %param.15) | copy-start | bytes 1572868
  33.5 30.4 %all-to-all-start.1 = ((bf16[64,8,512]{2,0,1:T(8,128)(2,1)}), bf16[64,8,512]{2,0,1:T(8,128)(2,1)S(1)}, u32[]{:S(2)}, u32[]{:S(2)}) async-start(bf16[64,8,512]{2,0,1:T(8,128)(2,1)} %copy.25), calls=%async_computation.1 | async-start | bytes 1048576 | tf_op jit(solution)/shard_map/all_to_all | solution.py:103
  43.2 30.7 %copy-start.5 = (bf16[1,64,4,1536]{3,2,1,0:T(4,128)(2,1)S(1)}, bf16[1,64,4,1536]{3,2,1,0:T(4,128)(2,1)}, u32[]{:S(2)}) copy-start(bf16[1,64,4,1536]{3,2,1,0:T(4,128)(2,1)} %param.16) | copy-start | bytes 2359300
  63.9 29.5 %copy-start.3 = (bf16[64,8,512]{2,0,1:T(8,128)(2,1)}, bf16[64,8,512]{2,0,1:T(8,128)(2,1)S(1)}, u32[]{:S(2)}) copy-start(bf16[64,8,512]{2,0,1:T(8,128)(2,1)S(1)} %all-to-all-done.1) | copy-start | bytes 1572868
  63.9 30.7 %all-to-all-start.3 = ((bf16[64,8,512]{2,0,1:T(8,128)(2,1)}), bf16[64,8,512]{2,0,1:T(8,128)(2,1)S(1)}, u32[]{:S(2)}, u32[]{:S(2)}) async-start(bf16[64,8,512]{2,0,1:T(8,128)(2,1)} %copy.27), calls=%async_computation.3 | async-start | bytes 1048576 | tf_op jit(solution)/shard_map/all_to_all | solution.py:104
  74.0 19.4 %copy-start.1 = (bf16[256,1536]{1,0:T(8,128)(2,1)}, bf16[256,1536]{1,0:T(8,128)(2,1)S(1)}, u32[]{:S(2)}) copy-start(bf16[256,1536]{1,0:T(8,128)(2,1)S(1)} %reshape_squeeze.2) | copy-start | bytes 2359300
  93.6 8.2 %copy-start.12 = (s32[1,4]{1,0:T(1,128)S(1)}, s32[1,4]{1,0:T(1,128)}, u32[]{:S(2)}) copy-start(s32[1,4]{1,0:T(1,128)} %param.19) | copy-start | bytes 52
  94.6 7.4 %copy-start.4 = (bf16[64,8,512]{2,0,1:T(8,128)(2,1)}, bf16[64,8,512]{2,0,1:T(8,128)(2,1)S(1)}, u32[]{:S(2)}) copy-start(bf16[64,8,512]{2,0,1:T(8,128)(2,1)S(1)} %all-to-all-done.3) | copy-start | bytes 1572868
  94.6 19.1 %all-to-all-start.2 = ((bf16[64,8,512]{2,0,1:T(8,128)(2,1)}), bf16[64,8,512]{2,0,1:T(8,128)(2,1)}, u32[]{:S(2)}, u32[]{:S(2)}) async-start(bf16[64,8,512]{2,0,1:T(8,128)(2,1)} %copy.26), calls=%async_computation.2 | async-start | bytes 1048576 | tf_op jit(solution)/shard_map/all_to_all | solution.py:105
  101.1 171.0 %all-gather.7.cloned.1.call-start = ((), (), s32[]{:S(2)}) async-start(), calls=%async_computation.8 | async-start | bytes 10616832 | tf_op jit(solution)/shard_map/all_gather | solution.py:145
  164.5 7.4 %copy-start.6 = (bf16[8,512,64]{1,2,0:T(8,128)(2,1)S(1)}, bf16[8,512,64]{1,2,0:T(8,128)(2,1)}, u32[]{:S(2)}) copy-start(bf16[8,512,64]{1,2,0:T(8,128)(2,1)} %get-tuple-element.82) | copy-start | bytes 1572868
  166.1 34.0 %all-to-all-start.4 = ((bf16[8,64,512]{2,1,0:T(8,128)(2,1)}), bf16[8,64,512]{2,1,0:T(8,128)(2,1)S(1)}, u32[]{:S(2)}, u32[]{:S(2)}) async-start(bf16[8,64,512]{2,1,0:T(8,128)(2,1)} %copy.38), calls=%async_computation.4 | async-start | bytes 1048576 | tf_op jit(solution)/shard_map/all_to_all | solution.py:131
  172.5 33.0 %copy-start.7 = (bf16[8,512,64]{1,2,0:T(8,128)(2,1)S(1)}, bf16[8,512,64]{1,2,0:T(8,128)(2,1)}, u32[]{:S(2)}) copy-start(bf16[8,512,64]{1,2,0:T(8,128)(2,1)} %get-tuple-element.83) | copy-start | bytes 1572868
  200.1 33.4 %all-to-all-start.5 = ((bf16[8,64,512]{2,1,0:T(8,128)(2,1)}), bf16[8,64,512]{2,1,0:T(8,128)(2,1)S(1)}, u32[]{:S(2)}, u32[]{:S(2)}) async-start(bf16[8,64,512]{2,1,0:T(8,128)(2,1)} %copy.39), calls=%async_computation.5 | async-start | bytes 1048576 | tf_op jit(solution)/shard_map/all_to_all | solution.py:132
  206.0 32.8 %copy-start = (bf16[1,64,4,1536]{3,2,1,0:T(4,128)(2,1)S(1)}, bf16[1,64,4,1536]{3,2,1,0:T(4,128)(2,1)}, u32[]{:S(2)}) copy-start(bf16[1,64,4,1536]{3,2,1,0:T(4,128)(2,1)} %param.11) | copy-start | bytes 2359300
  233.4 29.8 %all-to-all-start.6 = ((bf16[8,64,512]{2,1,0:T(8,128)(2,1)}), bf16[8,64,512]{2,1,0:T(8,128)(2,1)}, u32[]{:S(2)}, u32[]{:S(2)}) async-start(bf16[8,64,512]{2,1,0:T(8,128)(2,1)} %copy.40), calls=%async_computation.6 | async-start | bytes 1048576 | tf_op jit(solution)/shard_map/all_to_all | solution.py:133
  238.8 1.4 copy-start.11
  241.8 30.3 %copy-start.10 = (bf16[256,1024]{1,0:T(8,128)(2,1)S(1)}, bf16[256,1024]{1,0:T(8,128)(2,1)}, u32[]{:S(2)}) copy-start(bf16[256,1024]{1,0:T(8,128)(2,1)} %reshape.137) | copy-start | bytes 1572868
  265.6 13.3 %copy-start.2 = (bf16[256,1536]{1,0:T(8,128)(2,1)S(1)}, bf16[256,1536]{1,0:T(8,128)(2,1)}, u32[]{:S(2)}) copy-start(bf16[256,1536]{1,0:T(8,128)(2,1)} %copy-done.1) | copy-start | bytes 2359300
  279.7 11.5 %collective-permute-start = (bf16[1,64,4,1536]{3,2,1,0:T(4,128)(2,1)S(1)}, bf16[1,64,4,1536]{3,2,1,0:T(4,128)(2,1)S(1)}, u32[]{:S(2)}, u32[]{:S(2)}) collective-permute-start(bf16[1,64,4,1536]{3,2,1,0:T(4,128)(2,1)S(1)} %reshape.140), channel_id=1, source_target_pairs={{0,24},{8,0},{16,8},{24,16},{1,25},{9,1},{17,9},{25,17},{2,26},{10... | collective-permute-start | bytes 2359304 | tf_op jit(solution)/shard_map/ppermute | solution.py:18
Sparse Core Ops, SparseCore 0:
  9.5 80.9 all-gather.4
  104.1 167.9 all-gather.6
where the time goes:
time: 303 us; the launch traced here: 299 us
  waiting for transfers between devices  152 us (50%)
  matrix products  51.7 us (17%)
  starting transfers between devices  48.8 us (16%)
  local copies, waits for them, and re-layouts  26.7 us (9%)
  between operations  13.7 us (5%)
  other arithmetic  5.78 us (2%)
    all_to_all x1, waiting for transfers between devices, on_device(): lax.all_to_all(join_items(query_grad), 'seq', split_axis=0, concat_axis=1...  26.1 us
    all_to_all x1, waiting for transfers between devices, on_device(): lax.all_to_all(join_items(key_gradient), 'seq', split_axis=0, concat_axis...  25.9 us
    all_to_all x1, waiting for transfers between devices, on_device(): lax.all_to_all(join_items(value_grad), 'seq', split_axis=0, concat_axis=1...  21.3 us
    all_to_all x1, waiting for transfers between devices, on_device(): lax.all_to_all(frame_keys, 'seq', split_axis=1, concat_axis=0, tiled=True)  19.7 us
    all_to_all x1, waiting for transfers between devices, on_device(): lax.all_to_all(frame_queries, 'seq', split_axis=1, concat_axis=0, tiled=T...  17.5 us
    all_gather x1, waiting for transfers between devices, project_grad(): lax.all_gather(out_rows, 'seq', axis=0, tiled=True)  16.5 us
    dot_general x8, matrix products, step(): lax.dot_general(probs_low, grad_block, COL_DOT, preferred_element_type=jn...  14.8 us
    ppermute x1, waiting for transfers between devices, shifted(): lax.ppermute(shard, axis, [(i, (i + by) % count) for i in range(count)])  10.9 us
  transfers between devices with their start and end apart: 10, of which 9 were waited for; matrix products, arithmetic and copies ran while one was open for 25% of the time, Pallas kernels for 0%

commit v1 on v0

--- a/solution.py
+++ b/solution.py
@@ -1,6 +1,10 @@
+import functools
+
 import jax
 import jax.numpy as jnp
 from jax import lax
+from jax.experimental import pallas as pl
+from jax.experimental.pallas import tpu as pltpu
 from jax.sharding import PartitionSpec as P
 
 HEADS = 16
@@ -163,6 +167,456 @@
     return shifted(input_grad, "section", -1)
 
 
+def body(
+    dims,
+    length_ref,
+    li_ref,
+    q_ref,
+    k_ref,
+    v_ref,
+    og_ref,
+    ow_in,
+    w_in,
+    gain_ref,
+    out_ref,
+    xq,
+    xk,
+    xv,
+    xg,
+    g_send,
+    ow,
+    w,
+    joined,
+    part_send,
+    part_recv,
+    li_here,
+    og_here,
+    x_send_sem,
+    x_recv_sem,
+    ow_send_sem,
+    ow_side_sem,
+    ow_recv_sem,
+    w_send_sem,
+    w_side_sem,
+    w_recv_sem,
+    p_send_sem,
+    p_recv_sem,
+    s_send_sem,
+    s_recv_sem,
+    local_sem,
+):
+    n, sections, groups, parts, frames, cols = dims
+    pairs = cols // (2 * HS)
+    section = lax.axis_index("section")
+    me = lax.axis_index("seq")
+    group = me // parts
+    part = me % parts
+    before = (section + sections - 1) % sections
+    after = (section + 1) % sections
+
+    def remote(src, dst, send, recv, sec, dev):
+        return pltpu.make_async_remote_copy(
+            src_ref=src,
+            dst_ref=dst,
+            send_sem=send,
+            recv_sem=recv,
+            device_id=(sec, dev),
+            device_id_type=pl.DeviceIdType.MESH,
+        )
+
+    barrier = pltpu.get_barrier_semaphore()
+
+    def greet(sec, dev):
+        pl.semaphore_signal(
+            barrier, inc=1, device_id=(sec, dev), device_id_type=pl.DeviceIdType.MESH
+        )
+
+    for k in range(1, n):
+        greet(section, (me + k) % n)
+    for k in range(n):
+        greet(before, (me + k) % n)
+        greet(after, (me + k) % n)
+
+    heads = [(q_ref, xq), (k_ref, xk), (v_ref, xv), (g_send, xg)]
+
+    def own(t):
+        src, dst = heads[t]
+        return pltpu.make_async_copy(
+            src.at[group, :, pl.ds(pl.multiple_of(part * cols, cols), cols)],
+            dst.at[me],
+            local_sem.at[t],
+        )
+
+    def exchange(t, k):
+        src, dst = heads[t]
+        to = (me + k) % n
+        return remote(
+            src.at[to // parts, :, pl.ds(pl.multiple_of((to % parts) * cols, cols), cols)],
+            dst.at[me],
+            x_send_sem.at[t, k],
+            x_recv_sem.at[t, k],
+            section,
+            to,
+        )
+
+    local_ow = pltpu.make_async_copy(ow_in, ow.at[me], local_sem.at[4])
+    local_w = pltpu.make_async_copy(w_in.at[part], w.at[me], local_sem.at[5])
+    local_ow.start()
+    local_w.start()
+    for t in range(3):
+        own(t).start()
+    pl.semaphore_wait(barrier, 3 * n - 1)
+    local_ow.wait()
+
+    def ow_hop(slot, way, dev):
+        return remote(
+            ow.at[slot], ow.at[slot], ow_send_sem.at[way, slot], ow_recv_sem.at[slot], section, dev
+        )
+
+    def ow_side(slot, k):
+        return remote(
+            ow.at[slot],
+            ow.at[slot],
+            ow_side_sem.at[k, slot],
+            ow_recv_sem.at[slot],
+            section,
+            group * parts + (part + k) % parts,
+        )
+
+    def w_hop(slot, way, dev):
+        return remote(
+            w.at[slot], w.at[slot], w_send_sem.at[way, slot], w_recv_sem.at[slot], section, dev
+        )
+
+    def w_side(k):
+        other = (part + k) % parts
+        return remote(
+            w_in.at[other],
+            w.at[me],
+            w_side_sem.at[k],
+            w_recv_sem.at[me],
+            section,
+            group * parts + other,
+        )
+
+    def ways(origin, act):
+        @pl.when((origin <= group) & (group + 1 < groups))
+        def _():
+            act(0, me + parts)
+
+        @pl.when((origin >= group) & (group >= 1))
+        def _():
+            act(1, me - parts)
+
+    def ow_pass(origin):
+        slot = origin * parts + part
+        ways(origin, lambda way, dev: ow_hop(slot, way, dev).start())
+        for k in range(1, parts):
+            ow_side(slot, k).start()
+
+    def ow_arrive(origin):
+        @pl.when((origin >= 0) & (origin < groups))
+        def _():
+            slot = origin * parts + part
+            ow_hop(slot, 0, me).wait_recv()
+            ow_pass(origin)
+
+    def w_pass(origin):
+        @pl.when((origin >= 0) & (origin < groups))
+        def _():
+            for other in range(parts):
+                slot = origin * parts + other
+
+                @pl.when(slot != me)
+                def _():
+                    w_hop(slot, 0, me).wait_recv()
+
+                ways(origin, lambda way, dev: w_hop(slot, way, dev).start())
+
+    ow_pass(group)
+    shift_og = remote(og_ref, og_here, s_send_sem.at[0], s_recv_sem.at[0], before, me)
+    shift_li = remote(li_ref, li_here, s_send_sem.at[1], s_recv_sem.at[1], before, me)
+    for k in range(1, n):
+        exchange(0, k).start()
+    shift_og.start()
+    shift_li.start()
+    for s in range(1, groups):
+        ow_arrive(group - s)
+        ow_arrive(group + s)
+        if s == 1:
+            for t in (1, 2):
+                for k in range(1, n):
+                    exchange(t, k).start()
+    for k in range(1, parts):
+        w_side(k).start()
+    for origin in range(groups):
+        for k in range(1, parts):
+            ow_side(origin * parts + (part + k) % parts, k).wait_recv()
+
+    features = groups * parts
+    rows_here = ow.shape[1]
+
+    def project(i, carry):
+        weight = ow[pl.ds(2 * i, 2)].reshape(2 * rows_here, ow.shape[2])
+        result = lax.dot_general(
+            og_ref[...], weight, ROW_DOT, preferred_element_type=jnp.float32
+        ).astype(jnp.bfloat16)
+        g_send[:, :, pl.ds(pl.multiple_of(i * 2 * rows_here, 2 * rows_here), 2 * rows_here)] = (
+            result.reshape(groups, frames, 2 * rows_here)
+        )
+        return carry
+
+    lax.fori_loop(0, features // 2, project, 0)
+    own(3).start()
+    for k in range(1, n):
+        exchange(3, k).start()
+    local_w.wait()
+    w_pass(group)
+    for t in range(4):
+        own(t).wait()
+        for k in range(1, n):
+            exchange(t, k).wait_recv()
+
+    length = n * frames
+    valid = length_ref[0]
+    keys_ok = lax.broadcasted_iota(jnp.int32, (length, 1), 0) < valid
+    low_lanes = lax.broadcasted_iota(jnp.int32, (length, 2 * HS), 1) < HS
+    scale = HS ** (-0.5)
+
+    def attend(j, carry):
+        lanes = pl.ds(pl.multiple_of(j * 2 * HS, 2 * HS), 2 * HS)
+        queries, keys, values, grads = (
+            x[:, :, lanes].reshape(length, 2 * HS) for x in (xq, xk, xv, xg)
+        )
+        keys_across = keys.T
+        nothing = jnp.zeros_like(keys)
+        halves = []
+        for h in range(2):
+            mine = low_lanes if h == 0 else jnp.logical_not(low_lanes)
+            key_h = jnp.where(mine, keys, nothing)
+            value_h = jnp.where(mine, values, nothing)
+            scores = (
+                lax.dot_general(key_h, queries, ROW_DOT, preferred_element_type=jnp.float32)
+                * scale
+            )
+            scores = jnp.where(keys_ok, scores, MASKED)
+            weights = jnp.exp(scores - jnp.max(scores, axis=0, keepdims=True))
+            probs = weights * (1.0 / jnp.sum(weights, axis=0, keepdims=True))
+            grad_probs = lax.dot_general(
+                value_h, grads, ROW_DOT, preferred_element_type=jnp.float32
+            )
+            centre = jnp.sum(probs * grad_probs, axis=0, keepdims=True)
+            grad_scores = (probs * (grad_probs - centre)).astype(jnp.bfloat16)
+            value_grad = jnp.dot(
+                probs.astype(jnp.bfloat16), grads, preferred_element_type=jnp.float32
+            )
+            key_grad = jnp.dot(grad_scores, queries, preferred_element_type=jnp.float32)
+            query_grad = jnp.dot(
+                keys_across[h * HS : (h + 1) * HS], grad_scores, preferred_element_type=jnp.float32
+            )
+            halves.append((query_grad, key_grad, value_grad))
+        (query_0, key_0, value_0), (query_1, key_1, value_1) = halves
+        query_both = (jnp.concatenate([query_0, query_1], axis=0) * scale).T
+        key_both = jnp.where(low_lanes, key_0, key_1) * scale
+        value_both = jnp.where(low_lanes, value_0, value_1)
+        for t, both in enumerate((query_both, key_both, value_both)):
+            at = pl.multiple_of(t * cols + j * 2 * HS, 2 * HS)
+            joined[:, pl.ds(at, 2 * HS)] = both.astype(jnp.bfloat16)
+
+        @pl.when(j == pairs - 2)
+        def _():
+            w_pass(group - 1)
+            w_pass(group + 1)
+
+        return carry
+
+    if pairs < 2:
+        w_pass(group - 1)
+        w_pass(group + 1)
+    lax.fori_loop(0, pairs, attend, 0)
+
+    def part_copy(origin, to):
+        return remote(
+            part_send.at[origin, to],
+            part_recv.at[me, origin],
+            p_send_sem.at[origin, to],
+            p_recv_sem.at[me, origin],
+            before,
+            to,
+        )
+
+    def norm_block(i, carry):
+        s = (i + 1) // 2
+        origin = group + s * (1 - 2 * (i % 2))
+
+        @pl.when(i >= 3)
+        def _():
+            w_pass(origin)
+
+        @pl.when((origin >= 0) & (origin < groups))
+        def _():
+            weight = w[pl.ds(origin * parts, parts)].reshape(parts * w.shape[1], w.shape[2])
+            sums = lax.dot_general(
+                joined[...], weight, ROW_DOT, preferred_element_type=jnp.float32
+            )
+            sums = (sums * gain_ref[origin]).astype(jnp.bfloat16)
+            part_send[origin] = sums.reshape(n, frames, sums.shape[1])
+            for k in range(n):
+                part_copy(origin, (me + k) % n).start()
+
+        return carry
+
+    lax.fori_loop(0, 2 * groups - 1, norm_block, 0)
+
+    shift_og.wait_recv()
+    shift_li.wait_recv()
+    for src in range(n):
+        for origin in range(groups):
+            remote(
+                part_send.at[origin, 0],
+                part_recv.at[src, origin],
+                p_send_sem.at[origin, 0],
+                p_recv_sem.at[src, origin],
+                before,
+                me,
+            ).wait_recv()
+
+    width = li_here.shape[1]
+    block = part_recv.shape[3]
+
+    def finish(r, carry):
+        rows = pl.ds(pl.multiple_of(r * frames, frames), frames)
+        inputs = li_here[rows, :].astype(jnp.float32)
+        centered = inputs - jnp.sum(inputs, axis=1, keepdims=True) * (1.0 / width)
+        var = jnp.sum(centered * centered, axis=1, keepdims=True) * (1.0 / width)
+        deviation = 1.0 / jnp.sqrt(var + EPSILON)
+        normal = centered * deviation
+        scaled = []
+        for origin in range(groups):
+            total = part_recv[r * parts, origin].astype(jnp.float32)
+            for k in range(1, parts):
+                total = total + part_recv[r * parts + k, origin].astype(jnp.float32)
+            scaled.append(total)
+        scaled = jnp.concatenate(scaled, axis=1)
+        average = jnp.sum(scaled, axis=1, keepdims=True) * (1.0 / width)
+        along = jnp.sum(scaled * normal, axis=1, keepdims=True) * (1.0 / width)
+        branch = deviation * (scaled - average - normal * along)
+        out_ref[rows, :] = (og_here[rows, :].astype(jnp.float32) + branch).astype(jnp.bfloat16)
+        return carry
+
+    lax.fori_loop(0, groups, finish, 0)
+
+    for t in range(4):
+        for k in range(1, n):
+            exchange(t, k).wait_send()
+    for origin in range(groups):
+        slot = origin * parts + part
+        ways(origin, lambda way, dev: ow_hop(slot, way, dev).wait_send())
+        for k in range(1, parts):
+            ow_side(slot, k).wait_send()
+        for other in range(parts):
+            w_slot = origin * parts + other
+            ways(origin, lambda way, dev: w_hop(w_slot, way, dev).wait_send())
+        for to in range(n):
+            part_copy(origin, to).wait_send()
+    for k in range(1, parts):
+        w_side(k).wait_send()
+    shift_og.wait_send()
+    shift_li.wait_send()
+
+
+def on_device_fused(
+    layer_input,
+    norm_gain,
+    queries,
+    key_states,
+    value_states,
+    out_grad,
+    out_weight,
+    qkv_weight,
+    lengths,
+):
+    n = lax.axis_size("seq")
+    sections = lax.axis_size("section")
+    frames, records, features = queries.shape[1:]
+    width = out_grad.shape[3]
+    parts = n // records
+    cols = features // parts
+    ow_rows = out_weight.shape[1]
+    w_rows = qkv_weight.shape[1]
+    block = parts * w_rows
+    group = lax.axis_index("seq") // parts
+    length_here = lax.dynamic_slice(lengths[0], (group,), (1,))
+
+    def by_record(x):
+        return x[0].transpose(1, 0, 2)
+
+    flat_input = by_record(layer_input).reshape(records * frames, width)
+    flat_grad = by_record(out_grad).reshape(records * frames, width)
+    w_parts = (
+        qkv_weight[0]
+        .reshape(w_rows, 3, parts, cols)
+        .transpose(2, 0, 1, 3)
+        .reshape(parts, w_rows, 3 * cols)
+    )
+    gain = norm_gain[0].reshape(records, 1, block)
+    vmem = pl.BlockSpec(memory_space=pltpu.VMEM)
+    low = jnp.bfloat16
+    dma = pltpu.SemaphoreType.DMA
+    out = pl.pallas_call(
+        functools.partial(body, (n, sections, records, parts, frames, cols)),
+        out_shape=jax.ShapeDtypeStruct((records * frames, width), low),
+        in_specs=[pl.BlockSpec(memory_space=pltpu.SMEM)] + [vmem] * 8,
+        out_specs=vmem,
+        scratch_shapes=[pltpu.VMEM((n, frames, cols), low)] * 4
+        + [
+            pltpu.VMEM((records, frames, features), low),
+            pltpu.VMEM((n, ow_rows, width), low),
+            pltpu.VMEM((n, w_rows, 3 * cols), low),
+            pltpu.VMEM((n * frames, 3 * cols), low),
+            pltpu.VMEM((records, n, frames, block), low),
+            pltpu.VMEM((n, records, frames, block), low),
+            pltpu.VMEM((records * frames, width), low),
+            pltpu.VMEM((records * frames, width), low),
+            dma((4, n)),
+            dma((4, n)),
+            dma((2, n)),
+            dma((parts, n)),
+            dma((n,)),
+            dma((2, n)),
+            dma((parts,)),
+            dma((n,)),
+            dma((records, n)),
+            dma((n, records)),
+            dma((2,)),
+            dma((2,)),
+            dma((6,)),
+        ],
+        compiler_params=pltpu.CompilerParams(
+            collective_id=0, has_side_effects=True, vmem_limit_bytes=60 * 1024 * 1024
+        ),
+    )(
+        length_here,
+        flat_input,
+        by_record(queries),
+        by_record(key_states),
+        by_record(value_states),
+        flat_grad,
+        out_weight[0],
+        w_parts,
+        gain,
+    )
+    return out.reshape(records, frames, width).transpose(1, 0, 2)[None]
+
+
+def fits(mesh, records, features):
+    n = mesh.shape["seq"]
+    if n % records or mesh.shape["section"] < 2:
+        return False
+    parts = n // records
+    return features % (parts * 2 * HS) == 0 and n % 2 == 0
+
+
 def solution(mesh):
     in_specs = (
         P("section", "seq", None, None),
@@ -176,6 +630,15 @@
         P("section", None),
     )
     out_specs = P("section", "seq", None, None)
-    return jax.shard_map(
-        on_device, mesh=mesh, in_specs=in_specs, out_specs=out_specs, check_vma=False
-    )
+
+    def run(*arrays):
+        fused = fits(mesh, arrays[2].shape[2], arrays[2].shape[3])
+        return jax.shard_map(
+            on_device_fused if fused else on_device,
+            mesh=mesh,
+            in_specs=in_specs,
+            out_specs=out_specs,
+            check_vma=False,
+        )(*arrays)
+
+    return run

time: 303 us -> 217 us (0.72); the launches traced: 299 us -> 217 us
  Pallas kernels: 0 us -> 203 us
  waiting for transfers between devices: 152 us -> 0 us
  matrix products: 51.7 us -> 0 us
  starting transfers between devices: 48.8 us -> 0 us
  between operations: 13.7 us -> 0.04 us
  local copies, waits for them, and re-layouts: 26.7 us -> 13.9 us
  other arithmetic: 5.78 us -> 0 us
    pallas_call x0 -> x1, Pallas kernels: none -> 203 us  [on_device_fused(): pl.pallas_call(functools.partial(body, (n, sections, records, parts, fram...]
    all_to_all x7 -> x0, waiting for transfers between devices: 117 us -> none  [the longest x1 26.1 us: on_device(): lax.all_to_all(join_items(query_grad), 'seq', split_axis=0, concat_axis=1...]
    dot_general x42 -> x0, matrix products: 51.7 us -> none  [the longest x8 14.8 us: step(): lax.dot_general(probs_low, grad_block, COL_DOT, preferred_element_type=jn...]
    all_to_all x7 -> x0, starting transfers between devices: 48.2 us -> none  [the longest x1 9.93 us: on_device(): lax.all_to_all(frame_values, 'seq', split_axis=1, concat_axis=0, tiled=True)]
    all_gather x2 -> x0, waiting for transfers between devices: 23 us -> none  [the longest x1 16.5 us: project_grad(): lax.all_gather(out_rows, 'seq', axis=0, tiled=True)]
    all_to_all x17 -> x0, local copies, waits for them, and re-layouts: 14.7 us -> none  [the longest x3 3.51 us: on_device(): lax.all_to_all(join_items(query_grad), 'seq', split_axis=0, concat_axis=1...]
    ppermute x1 -> x0, waiting for transfers between devices: 10.9 us -> none  [shifted(): lax.ppermute(shard, axis, [(i, (i + by) % count) for i in range(count)])]
    transpose x0 -> x3, local copies, waits for them, and re-layouts: none -> 4.59 us  [by_record(): return x[0].transpose(1, 0, 2)]
  transfers between devices with their start and end apart: 10 -> 0, of which waited for: 9 -> 0; matrix products, arithmetic and copies ran while one was open for 25% -> 0% of each run, Pallas kernels for 0% -> 0%
where the time goes in v1:
time: 217 us
  Pallas kernels  203 us (94%)
  local copies, waits for them, and re-layouts  13.9 us (6%)
    pallas_call x1, Pallas kernels, on_device_fused(): pl.pallas_call(functools.partial(body, (n, sections, records, parts, fram...  203 us
    transpose x3, local copies, waits for them, and re-layouts, by_record(): return x[0].transpose(1, 0, 2)  4.59 us

profile of v1, /device:TPU:27, one launch (start us, length us, event | category | flops | bytes accessed | tf_op | source)
XLA Modules:
  0.0 216.8 jit_solution(2442094573493146479)
XLA Ops:
  0.0 0.0 copy-start
  0.0 0.0 copy-start.1
  0.0 0.7 copy-done
  0.7 0.6 constant_dynamic-slice_fusion
  1.3 2.5 %copy_bitcast_fusion.2 = (bf16[4,64,1024]{2,1,0:T(8,128)(2,1)}, bf16[4,64,1024]{2,1,0:T(8,128)(2,1)}) fusion(bf16[1,64,4,1024]{3,2,1,0:T(4,128)(2,1)} %param.13, bf16[1,64,4,1024]{3,2,1,0:T(4,128)(2,1)} %param.12), kind=kLoop, calls=%fused_computation.2 | loop fusion | bytes 2097152 | tf_op jit(solution)/shard_map/transpose | solution.py:552
  3.8 0.0 copy-done.1
  3.8 0.9 reshape_squeeze.6
  4.7 0.6 copy.29
  5.3 0.0 copy-start.2
  5.3 2.7 %reshape.15.w_in = bf16[2,192,1536]{2,1,0:T(8,128)(2,1)} reshape(bf16[2,192,3,512]{3,2,1,0:T(4,128)(2,1)S(1)} %bitcast.33) | data formatting | bytes 2359296 | tf_op jit(solution)/shard_map/reshape | solution.py:560
  8.0 0.0 copy-start.3
  8.0 0.0 copy-done.2
  8.0 1.1 copy.21
  9.1 0.0 copy-start.4
  9.1 0.3 copy-done.3
  9.3 1.0 copy.17
  10.4 0.0 copy-done.4
  10.4 1.0 copy.31
  11.3 202.9 %shard_map.91 = bf16[256,1536]{1,0:T(8,128)(2,1)} custom-call(s32[1]{0:T(128)} %bitcast.length_ref, bf16[256,1536]{1,0:T(8,128)(2,1)} %bitcast.36, bf16[4,64,1024]{2,1,0:T(8,128)(2,1)} %bitcast.37, bf16[4,64,1024]{2,1,0:T(8,128)(2,1)} %get-tuple-element.6.k_ref, bf16[4,64,1024]{2,1,0:T(8,128)(2,1)} %get-tuple-element.5.v_ref, bf16[256,1536]{1,0:T(8,128)(2,1)} %bitcast.35, ...), custom_call_target="tpu_custom_call" | custom-call | tf_op jit(solution)/shard_map/pallas_call | solution.py:566
  214.2 2.6 %copy.30 = bf16[4,64,1536]{2,0,1:T(4,128)(2,1)} copy(bf16[4,64,1536]{2,1,0:T(8,128)(2,1)} %bitcast.34) | data formatting | bytes 1572864 | tf_op jit(solution)/shard_map/reshape | solution.py:609
Async XLA Ops:
  0.0 0.7 copy-start
  0.0 3.8 %copy-start.1 = (bf16[1,192,3072]{2,1,0:T(8,128)(2,1)S(1)}, bf16[1,192,3072]{2,1,0:T(8,128)(2,1)}, u32[]{:S(2)}) copy-start(bf16[1,192,3072]{2,1,0:T(8,128)(2,1)} %param.16) | copy-start | bytes 3538948
  5.3 2.7 %copy-start.2 = (bf16[1,64,4,1536]{3,2,1,0:T(4,128)(2,1)S(1)}, bf16[1,64,4,1536]{3,2,1,0:T(4,128)(2,1)}, u32[]{:S(2)}) copy-start(bf16[1,64,4,1536]{3,2,1,0:T(4,128)(2,1)} %param.14) | copy-start | bytes 2359300
  8.0 1.3 copy-start.3
  9.1 1.3 copy-start.4

commit v2 on v1

--- a/solution.py
+++ b/solution.py
@@ -188,6 +188,8 @@
     w,
     joined,
     part_send,
+    side_recv,
+    sum_send,
     part_recv,
     li_here,
     og_here,
@@ -198,7 +200,10 @@
     ow_recv_sem,
     w_send_sem,
     w_side_sem,
+    w_near_sem,
     w_recv_sem,
+    side_send_sem,
+    side_recv_sem,
     p_send_sem,
     p_recv_sem,
     s_send_sem,
@@ -260,9 +265,18 @@
         )
 
     local_ow = pltpu.make_async_copy(ow_in, ow.at[me], local_sem.at[4])
-    local_w = pltpu.make_async_copy(w_in.at[part], w.at[me], local_sem.at[5])
+
+    def piece(t, which):
+        return w_in.at[:, pl.ds(pl.multiple_of((t * parts + which) * cols, cols), cols)]
+
+    def local_w(t):
+        return pltpu.make_async_copy(
+            piece(t, part), w.at[me, :, pl.ds(t * cols, cols)], local_sem.at[5 + t]
+        )
+
     local_ow.start()
-    local_w.start()
+    for t in range(3):
+        local_w(t).start()
     for t in range(3):
         own(t).start()
     pl.semaphore_wait(barrier, 3 * n - 1)
@@ -288,13 +302,13 @@
             w.at[slot], w.at[slot], w_send_sem.at[way, slot], w_recv_sem.at[slot], section, dev
         )
 
-    def w_side(k):
+    def w_side(t, k):
         other = (part + k) % parts
         return remote(
-            w_in.at[other],
-            w.at[me],
-            w_side_sem.at[k],
-            w_recv_sem.at[me],
+            piece(t, other),
+            w.at[me, :, pl.ds(t * cols, cols)],
+            w_side_sem.at[t, k],
+            w_near_sem.at[t, k],
             section,
             group * parts + other,
         )
@@ -326,12 +340,18 @@
         def _():
             for other in range(parts):
                 slot = origin * parts + other
-
-                @pl.when(slot != me)
-                def _():
-                    w_hop(slot, 0, me).wait_recv()
-
+                w_hop(slot, 0, me).wait_recv()
                 ways(origin, lambda way, dev: w_hop(slot, way, dev).start())
+
+    def w_first():
+        for t in range(3):
+            local_w(t).wait()
+        ways(group, lambda way, dev: w_hop(me, way, dev).start())
+        for k in range(1, parts):
+            for t in range(3):
+                w_side(t, k).wait_recv()
+            slot = group * parts + (part + parts - k) % parts
+            ways(group, lambda way, dev: w_hop(slot, way, dev).start())
 
     ow_pass(group)
     shift_og = remote(og_ref, og_here, s_send_sem.at[0], s_recv_sem.at[0], before, me)
@@ -348,7 +368,8 @@
                 for k in range(1, n):
                     exchange(t, k).start()
     for k in range(1, parts):
-        w_side(k).start()
+        for t in range(3):
+            w_side(t, k).start()
     for origin in range(groups):
         for k in range(1, parts):
             ow_side(origin * parts + (part + k) % parts, k).wait_recv()
@@ -370,8 +391,7 @@
     own(3).start()
     for k in range(1, n):
         exchange(3, k).start()
-    local_w.wait()
-    w_pass(group)
+    w_first()
     for t in range(4):
         own(t).wait()
         for k in range(1, n):
@@ -435,45 +455,74 @@
         w_pass(group + 1)
     lax.fori_loop(0, pairs, attend, 0)
 
-    def part_copy(origin, to):
+    def side_copy(origin, k):
+        other = (part + k) % parts
         return remote(
-            part_send.at[origin, to],
-            part_recv.at[me, origin],
+            part_send.at[origin, other],
+            side_recv.at[origin, k],
+            side_send_sem.at[origin, k],
+            side_recv_sem.at[origin, k],
+            section,
+            group * parts + other,
+        )
+
+    def sum_copy(origin, to):
+        return remote(
+            sum_send.at[origin, to],
+            part_recv.at[group, origin],
             p_send_sem.at[origin, to],
-            p_recv_sem.at[me, origin],
+            p_recv_sem.at[group, origin],
             before,
-            to,
-        )
+            to * parts + part,
+        )
+
+    blocks = 2 * groups - 1
+
+    def origin_of(i):
+        return group + ((i + 1) // 2) * (1 - 2 * (i % 2))
 
     def norm_block(i, carry):
-        s = (i + 1) // 2
-        origin = group + s * (1 - 2 * (i % 2))
-
-        @pl.when(i >= 3)
+        earlier = origin_of(i - 2)
+
+        @pl.when((i >= 2) & (earlier >= 0) & (earlier < groups))
+        def _():
+            total = part_send[earlier, part].astype(jnp.float32)
+            for k in range(1, parts):
+                side_copy(earlier, k).wait_recv()
+                total = total + side_recv[earlier, k].astype(jnp.float32)
+            sum_send[earlier] = total.astype(jnp.bfloat16)
+            for k in range(groups):
+                sum_copy(earlier, (group + k) % groups).start()
+
+        origin = origin_of(i)
+
+        @pl.when((i >= 3) & (i < blocks))
         def _():
             w_pass(origin)
 
-        @pl.when((origin >= 0) & (origin < groups))
+        @pl.when((i < blocks) & (origin >= 0) & (origin < groups))
         def _():
             weight = w[pl.ds(origin * parts, parts)].reshape(parts * w.shape[1], w.shape[2])
             sums = lax.dot_general(
                 joined[...], weight, ROW_DOT, preferred_element_type=jnp.float32
             )
             sums = (sums * gain_ref[origin]).astype(jnp.bfloat16)
-            part_send[origin] = sums.reshape(n, frames, sums.shape[1])
-            for k in range(n):
-                part_copy(origin, (me + k) % n).start()
+            sums = sums.reshape(groups, parts, frames, sums.shape[1])
+            for other in range(parts):
+                part_send[origin, other] = sums[:, other]
+            for k in range(1, parts):
+                side_copy(origin, k).start()
 
         return carry
 
-    lax.fori_loop(0, 2 * groups - 1, norm_block, 0)
+    lax.fori_loop(0, blocks + 2, norm_block, 0)
 
     shift_og.wait_recv()
     shift_li.wait_recv()
-    for src in range(n):
+    for src in range(groups):
         for origin in range(groups):
             remote(
-                part_send.at[origin, 0],
+                sum_send.at[origin, 0],
                 part_recv.at[src, origin],
                 p_send_sem.at[origin, 0],
                 p_recv_sem.at[src, origin],
@@ -482,7 +531,6 @@
             ).wait_recv()
 
     width = li_here.shape[1]
-    block = part_recv.shape[3]
 
     def finish(r, carry):
         rows = pl.ds(pl.multiple_of(r * frames, frames), frames)
@@ -493,10 +541,7 @@
         normal = centered * deviation
         scaled = []
         for origin in range(groups):
-            total = part_recv[r * parts, origin].astype(jnp.float32)
-            for k in range(1, parts):
-                total = total + part_recv[r * parts + k, origin].astype(jnp.float32)
-            scaled.append(total)
+            scaled.append(part_recv[r, origin].astype(jnp.float32))
         scaled = jnp.concatenate(scaled, axis=1)
         average = jnp.sum(scaled, axis=1, keepdims=True) * (1.0 / width)
         along = jnp.sum(scaled * normal, axis=1, keepdims=True) * (1.0 / width)
@@ -517,10 +562,13 @@
         for other in range(parts):
             w_slot = origin * parts + other
             ways(origin, lambda way, dev: w_hop(w_slot, way, dev).wait_send())
-        for to in range(n):
-            part_copy(origin, to).wait_send()
+        for to in range(groups):
+            sum_copy(origin, to).wait_send()
+        for k in range(1, parts):
+            side_copy(origin, k).wait_send()
     for k in range(1, parts):
-        w_side(k).wait_send()
+        for t in range(3):
+            w_side(t, k).wait_send()
     shift_og.wait_send()
     shift_li.wait_send()
 
@@ -553,12 +601,6 @@
 
     flat_input = by_record(layer_input).reshape(records * frames, width)
     flat_grad = by_record(out_grad).reshape(records * frames, width)
-    w_parts = (
-        qkv_weight[0]
-        .reshape(w_rows, 3, parts, cols)
-        .transpose(2, 0, 1, 3)
-        .reshape(parts, w_rows, 3 * cols)
-    )
     gain = norm_gain[0].reshape(records, 1, block)
     vmem = pl.BlockSpec(memory_space=pltpu.VMEM)
     low = jnp.bfloat16
@@ -574,8 +616,10 @@
             pltpu.VMEM((n, ow_rows, width), low),
             pltpu.VMEM((n, w_rows, 3 * cols), low),
             pltpu.VMEM((n * frames, 3 * cols), low),
-            pltpu.VMEM((records, n, frames, block), low),
-            pltpu.VMEM((n, records, frames, block), low),
+            pltpu.VMEM((records, parts, records, frames, block), low),
+            pltpu.VMEM((records, parts, records, frames, block), low),
+            pltpu.VMEM((records, records, frames, block), low),
+            pltpu.VMEM((records, records, frames, block), low),
             pltpu.VMEM((records * frames, width), low),
             pltpu.VMEM((records * frames, width), low),
             dma((4, n)),
@@ -584,13 +628,16 @@
             dma((parts, n)),
             dma((n,)),
             dma((2, n)),
-            dma((parts,)),
+            dma((3, parts)),
+            dma((3, parts)),
             dma((n,)),
-            dma((records, n)),
-            dma((n, records)),
+            dma((records, parts)),
+            dma((records, parts)),
+            dma((records, records)),
+            dma((records, records)),
             dma((2,)),
             dma((2,)),
-            dma((6,)),
+            dma((8,)),
         ],
         compiler_params=pltpu.CompilerParams(
             collective_id=0, has_side_effects=True, vmem_limit_bytes=60 * 1024 * 1024
@@ -603,7 +650,7 @@
         by_record(value_states),
         flat_grad,
         out_weight[0],
-        w_parts,
+        qkv_weight[0],
         gain,
     )
     return out.reshape(records, frames, width).transpose(1, 0, 2)[None]

time: 217 us -> 200 us (0.922)
  Pallas kernels: 203 us -> 190 us
  local copies, waits for them, and re-layouts: 13.9 us -> 9.79 us
    pallas_call x1, Pallas kernels: 203 us -> 190 us  [on_device_fused(): pl.pallas_call(functools.partial(body, (n, sections, records, parts, fram...]
    reshape x1 -> x0, local copies, waits for them, and re-layouts: 2.65 us -> none  [on_device_fused(): w_parts = qkv_weight[0].reshape(w_rows, 3, parts, cols).transpose(2, 0, 1...]
where the time goes in v2:
time: 200 us
  Pallas kernels  190 us (95%)
  local copies, waits for them, and re-layouts  9.79 us (5%)
    pallas_call x1, Pallas kernels, on_device_fused(): pl.pallas_call(functools.partial(body, (n, sections, records, parts, fram...  190 us

profile of v2, /device:TPU:27, one launch (start us, length us, event | category | flops | bytes accessed | tf_op | source)
XLA Modules:
  0.0 200.2 jit_solution(17297284743752061422)
XLA Ops:
  0.0 0.0 copy-start
  0.0 0.0 copy-start.1
  0.0 0.7 copy-done
  0.7 0.7 constant_dynamic-slice_fusion
  1.3 0.0 copy-start.2
  1.3 2.1 %copy.21 = bf16[1,64,4,1024]{3,1,2,0:T(8,128)(2,1)} copy(bf16[1,64,4,1024]{3,2,1,0:T(4,128)(2,1)} %param.11) | data formatting | bytes 1048576 | tf_op args[2]
  3.4 0.0 copy-done.1
  3.4 1.0 copy.10
  4.4 0.0 copy-start.3
  4.4 0.0 copy-start.4
  4.4 0.0 copy-done.2
  4.4 1.0 copy.14
  5.4 0.0 copy-done.3
  5.4 0.4 copy-done.4
  5.9 1.3 copy_bitcast_fusion.1
  7.2 190.4 %shard_map.91 = bf16[256,1536]{1,0:T(8,128)(2,1)} custom-call(s32[1]{0:T(128)} %bitcast.length_ref, bf16[256,1536]{1,0:T(8,128)(2,1)} %bitcast.31, bf16[4,64,1024]{2,1,0:T(8,128)(2,1)} %bitcast.34, bf16[4,64,1024]{2,1,0:T(8,128)(2,1)} %get-tuple-element.6.k_ref, bf16[4,64,1024]{2,1,0:T(8,128)(2,1)} %get-tuple-element.5.v_ref, bf16[256,1536]{1,0:T(8,128)(2,1)} %bitcast.32, ...), custom_call_target="tpu_custom_call" | custom-call | tf_op jit(solution)/shard_map/pallas_call | solution.py:608
  197.6 2.6 %copy.20 = bf16[4,64,1536]{2,0,1:T(4,128)(2,1)} copy(bf16[4,64,1536]{2,1,0:T(8,128)(2,1)} %bitcast.33) | data formatting | bytes 1572864 | tf_op jit(solution)/shard_map/reshape | solution.py:656
Async XLA Ops:
  0.0 0.7 copy-start
  0.0 3.4 %copy-start.1 = (bf16[1,64,4,1536]{3,2,1,0:T(4,128)(2,1)S(1)}, bf16[1,64,4,1536]{3,2,1,0:T(4,128)(2,1)}, u32[]{:S(2)}) copy-start(bf16[1,64,4,1536]{3,2,1,0:T(4,128)(2,1)} %param.9) | copy-start | bytes 2359300
  1.3 3.1 %copy-start.2 = (bf16[1,64,4,1536]{3,2,1,0:T(4,128)(2,1)S(1)}, bf16[1,64,4,1536]{3,2,1,0:T(4,128)(2,1)}, u32[]{:S(2)}) copy-start(bf16[1,64,4,1536]{3,2,1,0:T(4,128)(2,1)} %param.14) | copy-start | bytes 2359300
  4.4 1.0 copy-start.3
  4.4 1.5 copy-start.4

commit v3 on v2

--- a/solution.py
+++ b/solution.py
@@ -363,13 +363,13 @@
     for s in range(1, groups):
         ow_arrive(group - s)
         ow_arrive(group + s)
-        if s == 1:
-            for t in (1, 2):
-                for k in range(1, n):
-                    exchange(t, k).start()
     for k in range(1, parts):
         for t in range(3):
             w_side(t, k).start()
+    for t in (1, 2):
+        for k in range(1, n):
+            exchange(t, k).start()
+    w_first()
     for origin in range(groups):
         for k in range(1, parts):
             ow_side(origin * parts + (part + k) % parts, k).wait_recv()
@@ -391,7 +391,8 @@
     own(3).start()
     for k in range(1, n):
         exchange(3, k).start()
-    w_first()
+    w_pass(group - 1)
+    w_pass(group + 1)
     for t in range(4):
         own(t).wait()
         for k in range(1, n):
@@ -445,14 +446,14 @@
 
         @pl.when(j == pairs - 2)
         def _():
-            w_pass(group - 1)
-            w_pass(group + 1)
+            w_pass(group - 2)
+            w_pass(group + 2)
 
         return carry
 
     if pairs < 2:
-        w_pass(group - 1)
-        w_pass(group + 1)
+        w_pass(group - 2)
+        w_pass(group + 2)
     lax.fori_loop(0, pairs, attend, 0)
 
     def side_copy(origin, k):
@@ -496,7 +497,7 @@
 
         origin = origin_of(i)
 
-        @pl.when((i >= 3) & (i < blocks))
+        @pl.when((i >= 5) & (i < blocks))
         def _():
             w_pass(origin)
 
@@ -530,11 +531,11 @@
                 me,
             ).wait_recv()
 
-    width = li_here.shape[1]
-
-    def finish(r, carry):
-        rows = pl.ds(pl.multiple_of(r * frames, frames), frames)
-        inputs = li_here[rows, :].astype(jnp.float32)
+    width = og_here.shape[1]
+
+    def finish(r):
+        rows = pl.ds(r * frames, frames)
+        inputs = li_here[:, r, :].astype(jnp.float32)
         centered = inputs - jnp.sum(inputs, axis=1, keepdims=True) * (1.0 / width)
         var = jnp.sum(centered * centered, axis=1, keepdims=True) * (1.0 / width)
         deviation = 1.0 / jnp.sqrt(var + EPSILON)
@@ -547,9 +548,9 @@
         along = jnp.sum(scaled * normal, axis=1, keepdims=True) * (1.0 / width)
         branch = deviation * (scaled - average - normal * along)
         out_ref[rows, :] = (og_here[rows, :].astype(jnp.float32) + branch).astype(jnp.bfloat16)
-        return carry
-
-    lax.fori_loop(0, groups, finish, 0)
+
+    for r in range(groups):
+        finish(r)
 
     for t in range(4):
         for k in range(1, n):
@@ -599,7 +600,7 @@
     def by_record(x):
         return x[0].transpose(1, 0, 2)
 
-    flat_input = by_record(layer_input).reshape(records * frames, width)
+    flat_input = layer_input[0]
     flat_grad = by_record(out_grad).reshape(records * frames, width)
     gain = norm_gain[0].reshape(records, 1, block)
     vmem = pl.BlockSpec(memory_space=pltpu.VMEM)
@@ -620,7 +621,7 @@
             pltpu.VMEM((records, parts, records, frames, block), low),
             pltpu.VMEM((records, records, frames, block), low),
             pltpu.VMEM((records, records, frames, block), low),
-            pltpu.VMEM((records * frames, width), low),
+            pltpu.VMEM((frames, records, width), low),
             pltpu.VMEM((records * frames, width), low),
             dma((4, n)),
             dma((4, n)),

time: 200 us -> 181 us (0.905)
  Pallas kernels: 190 us -> 173 us
    pallas_call x1, Pallas kernels: 190 us -> 173 us  [on_device_fused(): pl.pallas_call(functools.partial(body, (n, sections, records, parts, fram...]
where the time goes in v3:
time: 181 us
  Pallas kernels  173 us (96%)
  local copies, waits for them, and re-layouts  8.25 us (5%)
    pallas_call x1, Pallas kernels, on_device_fused(): pl.pallas_call(functools.partial(body, (n, sections, records, parts, fram...  173 us

profile of v3, /device:TPU:27, one launch (start us, length us, event | category | flops | bytes accessed | tf_op | source)
XLA Modules:
  0.0 181.2 jit_solution(15574433382834262160)
XLA Ops:
  0.0 0.0 copy-start
  0.0 0.0 copy-start.1
  0.0 0.7 copy-done
  0.7 0.6 constant_dynamic-slice_fusion
  1.2 0.0 copy-start.2
  1.2 0.0 copy-start.3
  1.2 2.1 %copy.20 = bf16[1,64,4,1024]{3,1,2,0:T(8,128)(2,1)} copy(bf16[1,64,4,1024]{3,2,1,0:T(4,128)(2,1)} %param.11) | data formatting | bytes 1048576 | tf_op args[2]
  3.3 0.0 copy-done.1
  3.3 1.0 copy.13
  4.3 0.0 copy-done.2
  4.3 0.0 copy-done.3
  4.3 1.3 copy_bitcast_fusion.1
  5.6 172.9 %shard_map.91 = bf16[256,1536]{1,0:T(8,128)(2,1)} custom-call(s32[1]{0:T(128)} %bitcast.length_ref, bf16[64,4,1536]{2,1,0:T(4,128)(2,1)} %bitcast.32, bf16[4,64,1024]{2,1,0:T(8,128)(2,1)} %bitcast.30, bf16[4,64,1024]{2,1,0:T(8,128)(2,1)} %get-tuple-element.6.k_ref, bf16[4,64,1024]{2,1,0:T(8,128)(2,1)} %get-tuple-element.5.v_ref, bf16[256,1536]{1,0:T(8,128)(2,1)} %bitcast.28, ...), custom_call_target="tpu_custom_call" | custom-call | tf_op jit(solution)/shard_map/pallas_call | solution.py:609
  178.6 2.6 %copy.19 = bf16[4,64,1536]{2,0,1:T(4,128)(2,1)} copy(bf16[4,64,1536]{2,1,0:T(8,128)(2,1)} %bitcast.29) | data formatting | bytes 1572864 | tf_op jit(solution)/shard_map/reshape | solution.py:657
Async XLA Ops:
  0.0 0.7 copy-start
  0.0 3.3 %copy-start.1 = (bf16[1,64,4,1536]{3,2,1,0:T(4,128)(2,1)S(1)}, bf16[1,64,4,1536]{3,2,1,0:T(4,128)(2,1)}, u32[]{:S(2)}) copy-start(bf16[1,64,4,1536]{3,2,1,0:T(4,128)(2,1)} %param.14) | copy-start | bytes 2359300
  1.2 3.1 %copy-start.2 = (bf16[1,64,4,1024]{3,2,1,0:T(4,128)(2,1)S(1)}, bf16[1,64,4,1024]{3,2,1,0:T(4,128)(2,1)}, u32[]{:S(2)}) copy-start(bf16[1,64,4,1024]{3,2,1,0:T(4,128)(2,1)} %param.13) | copy-start | bytes 1572868
  1.2 3.1 %copy-start.3 = (bf16[1,64,4,1024]{3,2,1,0:T(4,128)(2,1)S(1)}, bf16[1,64,4,1024]{3,2,1,0:T(4,128)(2,1)}, u32[]{:S(2)}) copy-start(bf16[1,64,4,1024]{3,2,1,0:T(4,128)(2,1)} %param.12) | copy-start | bytes 1572868
